TPU v7x, 256 devices: a whole 4x4x8 slice. The times are simulated.
256 devices in a mesh: grp: 4 (over x), tok: 16 (over z, core), mdl: 4 (over y).
Axes of the slice: x: 4, y: 4, z: 8, core: 2. Of those that a mesh axis runs over, the one named last changes fastest.
Arguments:
- hidden_in: bfloat16 [4, 4096, 2048], P('grp', 'tok', 'mdl'), may hold values from -6 to 6
- suffix_len: int32 [4], P('grp'), may hold values from 512 to 4096, as said below
- norm_gain: bfloat16 [2048], replicated, may hold values from 0.099609375 to 1.8984375
- w_query: bfloat16 [2048, 2048], P(('grp', 'tok'), 'mdl'), may hold values from -0.5 to 0.5
- w_key: bfloat16 [2048, 512], P(('grp', 'tok'), 'mdl'), may hold values from -0.5 to 0.5
- w_value: bfloat16 [2048, 512], P(('grp', 'tok'), 'mdl'), may hold values from -0.125 to 0.125
- w_out: bfloat16 [2048, 2048], P(('grp', 'tok'), 'mdl'), may hold values from -0.5 to 0.5
- sink_logits: float32 [32], P('mdl'), may hold values from 8 to 12
- prefix_keys: bfloat16 [4, 4096, 512], P('grp', 'tok', 'mdl'), may hold values from -280 to 280
- prefix_values: bfloat16 [4, 4096, 512], P('grp', 'tok', 'mdl'), may hold values from -6 to 6
Outputs:
- attn_out: bfloat16 [4, 4096, 2048], P('grp', 'tok', 'mdl')
Inputs may be any that keep to these rules, and one draw needn't show every extreme that they name: `suffix_len`: one group in every draw has all 4096 slots live.
All inputs are finite; a program needn't handle non-finite values.
Results may differ from a plain program's by a relative error of at most 0.015.
The roundings to bfloat16 on the way count: a program that leaves them out, or rounds other values in their place, can miss the bound.
Values may be sent and summed in bfloat16 or wider, within the bound.
No kernel may reach another device: no remote copies, remote signals or barrier semaphores. Data moves between devices by JAX's collectives and lax.ppermute only.
A program may use at most 64 MiB of HBM per device.

v0:
```python
import jax
import jax.numpy as jnp
from jax import lax
from jax.sharding import PartitionSpec as P

HD = 64
SCORE_SCALE = 0.015625
EPSILON = 1e-05
LOG_THETA = 16.11809565095832


def rotate(heads_in, positions):
    half_dim = heads_in.shape[-1] // 2
    frequency = jnp.exp(
        -LOG_THETA * 2.0 * jnp.arange(half_dim, dtype=jnp.float32) / heads_in.shape[-1]
    )
    angles = positions[:, None] * frequency[None, :]
    cosine = jnp.concatenate([jnp.cos(angles), jnp.cos(angles)], axis=-1)[:, None, :]
    sine_part = jnp.concatenate([jnp.sin(angles), jnp.sin(angles)], axis=-1)[:, None, :]
    turned = jnp.concatenate([-heads_in[..., half_dim:], heads_in[..., :half_dim]], axis=-1)
    return heads_in * cosine + turned * sine_part


def on_device(
    hidden_in,
    suffix_len,
    norm_gain,
    w_query,
    w_key,
    w_value,
    w_out,
    sink_logits,
    prefix_keys,
    prefix_values,
):
    group_count, tok_rows, _ = hidden_in.shape
    head_count = sink_logits.shape[0]
    kv_width = prefix_keys.shape[2]
    kv_heads = kv_width // HD
    repeat = head_count // kv_heads
    tok_count = lax.axis_size("tok")
    own_index = lax.axis_index("tok")
    seq_span = tok_rows * tok_count
    gathered = lax.all_gather(hidden_in, "mdl", axis=2, tiled=True)
    features = gathered.astype(jnp.float32)
    normed = (
        features
        * lax.rsqrt(jnp.mean(features * features, axis=-1, keepdims=True) + EPSILON)
        * norm_gain.astype(jnp.float32)
    ).astype(jnp.bfloat16)
    normed = normed.reshape(group_count * tok_rows, -1)
    shard_rows = (
        lax.all_gather(w_query, ("grp", "tok"), axis=0, tiled=True),
        lax.all_gather(w_key, ("grp", "tok"), axis=0, tiled=True),
        lax.all_gather(w_value, ("grp", "tok"), axis=0, tiled=True),
    )
    query_sums, key_sums, value_sums = tuple(
        (
            jnp.dot(normed, weight_rows, preferred_element_type=jnp.float32)
            for weight_rows in shard_rows
        )
    )
    local_slots = own_index * tok_rows + jnp.arange(tok_rows, dtype=jnp.int32)
    query_pos = seq_span + local_slots
    positions = query_pos.astype(jnp.float32)
    queries = rotate(query_sums.reshape(group_count, tok_rows, head_count, HD), positions).astype(
        jnp.bfloat16
    )
    query_groups = queries.reshape(group_count, tok_rows, kv_heads, repeat, HD)
    new_keys = rotate(key_sums.reshape(group_count, tok_rows, kv_heads, HD), positions).astype(
        jnp.bfloat16
    )
    new_values = value_sums.astype(jnp.bfloat16).reshape(group_count, tok_rows, kv_width)
    kv_new = jnp.concatenate(
        [new_keys.reshape(group_count, tok_rows, kv_width), new_values], axis=2
    )
    kv_prefix = jnp.concatenate([prefix_keys, prefix_values], axis=2)

    def attend_part(softmax_state, key_block, key_pos):
        row_top, denoms, weighted = softmax_state
        key_count = key_block.shape[1]
        key_rows = key_block[..., :kv_width].reshape(group_count, key_count, kv_heads, HD)
        value_rows = key_block[..., kv_width:].reshape(group_count, key_count, kv_heads, HD)
        scores = (
            jnp.einsum(
                "gbkrh,gskh->gkrbs", query_groups, key_rows, preferred_element_type=jnp.float32
            )
            * SCORE_SCALE
        )
        allowed = (key_pos[None, :] <= query_pos[:, None]) & (
            key_pos[None, :] > query_pos[:, None] - seq_span
        )
        scores = jnp.where(allowed, scores, -jnp.inf)
        new_top = jnp.maximum(row_top, jnp.max(scores, axis=-1))
        expo_terms = jnp.where(allowed, jnp.exp(scores - new_top[..., None]), 0.0)
        rescale = jnp.exp(row_top - new_top)
        denoms = denoms * rescale + jnp.sum(expo_terms, axis=-1)
        weighted = weighted * rescale[..., None] + jnp.einsum(
            "gkrbs,gskh->gkrbh",
            expo_terms.astype(jnp.bfloat16),
            value_rows,
            preferred_element_type=jnp.float32,
        )
        return (new_top, denoms, weighted)

    def attend(softmax_state, key_block, key_pos):
        key_count = key_block.shape[1]
        block_count = key_count // 512
        blocks = jnp.swapaxes(
            key_block.reshape(group_count, block_count, 512, key_block.shape[2]), 0, 1
        )
        block_pos = key_pos.reshape(block_count, 512)

        def scan_step(inner_state, inputs):
            return (attend_part(inner_state, inputs[0], inputs[1]), None)

        final_state, _ = lax.scan(scan_step, softmax_state, (blocks, block_pos))
        return final_state

    sinks = sink_logits.reshape(1, kv_heads, repeat, 1)
    state_shape = (group_count, kv_heads, repeat, tok_rows)
    initial_state = (
        jnp.broadcast_to(sinks, state_shape),
        jnp.ones(state_shape, jnp.float32),
        jnp.zeros(state_shape + (HD,), jnp.float32),
    )
    softmax_state = initial_state
    shard_pair = (
        lax.all_gather(kv_prefix, "tok", axis=1, tiled=True),
        lax.all_gather(kv_new, "tok", axis=1, tiled=True),
    )
    row_count = shard_pair[0].shape[1]
    offsets = jnp.arange(row_count, dtype=jnp.int32)
    softmax_state = attend(softmax_state, shard_pair[0], offsets)
    final_state = attend(softmax_state, shard_pair[1], seq_span + offsets)
    row_top, denoms, weighted = final_state
    mixed = weighted / denoms[..., None]
    mixed = jnp.transpose(mixed, (0, 3, 1, 2, 4)).reshape(group_count, tok_rows, head_count * HD)
    live = local_slots[None, :] < suffix_len[:, None]
    mixed = jnp.where(live[..., None], mixed, 0.0).astype(jnp.bfloat16)
    mixed_rows = mixed.reshape(group_count * tok_rows, head_count * HD)
    partial_out = lax.dot_general(
        mixed_rows,
        lax.all_gather(w_out, ("grp", "tok"), axis=0, tiled=True),
        (((1,), (1,)), ((), ())),
        preferred_element_type=jnp.float32,
    )
    partial_out = partial_out.reshape(group_count, tok_rows, -1)
    summed = lax.psum_scatter(
        partial_out.astype(jnp.bfloat16), "mdl", scatter_dimension=2, tiled=True
    )
    return summed


def solution(mesh):
    placed = (
        P("grp", "tok", "mdl"),
        P("grp"),
        P(),
        P(("grp", "tok"), "mdl"),
        P(("grp", "tok"), "mdl"),
        P(("grp", "tok"), "mdl"),
        P(("grp", "tok"), "mdl"),
        P("mdl"),
        P("grp", "tok", "mdl"),
        P("grp", "tok", "mdl"),
    )
    return jax.shard_map(
        on_device, mesh=mesh, in_specs=placed, out_specs=P("grp", "tok", "mdl"), check_vma=False
    )
```

profile of v0, /device:TPU:2, one launch (start us, length us, event | category | flops | bytes accessed | tf_op | source)
XLA Modules:
  0.0 312.6 jit_solution(16367372434368591461)
XLA Ops:
  8.1 1.5 pad_maximum_fusion
  10.6 52.9 %all_gather.25 = bf16[2048,128]{1,0:T(8,128)(2,1)S(1)} all-gather(bf16[32,128]{1,0:T(8,128)(2,1)} %param.19), channel_id=1, replica_groups=mesh['grp'=4,'tok'=16,'mdl'=4] {'grp','tok'}, dimensions={0}, use_global_device_ids=true | all-gather | bytes 532480 | tf_op jit(solution)/shard_map/all_gather | solution.py:55
  63.5 48.3 %all_gather.24 = bf16[2048,128]{1,0:T(8,128)(2,1)S(1)} all-gather(bf16[32,128]{1,0:T(8,128)(2,1)} %param.18), channel_id=1, replica_groups=mesh['grp'=4,'tok'=16,'mdl'=4] {'grp','tok'}, dimensions={0}, use_global_device_ids=true | all-gather | bytes 532480 | tf_op jit(solution)/shard_map/all_gather | solution.py:54
  111.8 1.6 fusion.43
  113.4 1.8 fusion.55
  118.2 2.6 fusion.57
  121.0 37.4 %all-gather.6.cloned.1.call-done = bf16[1,4096,256]{2,1,0:T(8,128)(2,1)} async-done(((bf16[1,256,256]{2,1,0:T(8,128)(2,1)}), bf16[1,4096,256]{2,1,0:T(8,128)(2,1)}) %all-gather.6.cloned.1.call-update) | async-done | bytes 2097168 | tf_op jit(solution)/shard_map/all_gather | solution.py:129
  158.5 68.9 %while.35 = (s32[]{:T(128)}, f32[1,2,4,256]{3,2,1,0:T(4,128)S(1)}, f32[1,2,4,256]{3,2,1,0:T(4,128)S(1)}, f32[1,2,4,256,64]{3,4,2,1,0:T(8,128)S(1)}, s32[8,512]{1...) while((s32[]{:T(128)}, f32[1,2,4,256]{3,2,1,0:T(4,128)S(1)}, ...), condition=%wide.region_4.5_spmd.clone, body=%wide.region_1.4_spmd.clone.sunk | while | flops 282862080 | bytes 33171616 | solution.py:117
  160.7 1.9 copy-done
  162.6 1.0 fusion.100
  163.7 3.4 %fusion.101 = f32[1,2,4,256,64]{3,4,2,1,0:T(8,128)S(1)} fusion(bf16[512,2,64,1]{0,2,3,1:T(8,128)(2,1)S(1)} %bitcast.229, f32[2,512,256,4]{2,1,3,0:T(8,128)} %copy-done, f32[2,4,256]{2,1,0:T(4,128)S(1)} %bitcast.228, pred[256,512]{0,1:T(8,128)(4,1)S(1)} %compare_and_fusion.5, f32[1,2,4,256,64]{3,4,2,1,0:T(8,128)S(1)} %get-tuple-element.487, ...), kind=kOutput, calls=%fused_computation.35.clone.1 | convolution fusion | flops 139853824 | bytes 5521409 | tf_op jit(solution)/shard_map/while/body/eval_jaxpr/gkrbs,gskh->gkrbh/dot_general | solution.py:98
  169.3 1.9 copy-done
  171.2 1.0 fusion.100
  172.3 3.4 %fusion.101 = f32[1,2,4,256,64]{3,4,2,1,0:T(8,128)S(1)} fusion(bf16[512,2,64,1]{0,2,3,1:T(8,128)(2,1)S(1)} %bitcast.229, f32[2,512,256,4]{2,1,3,0:T(8,128)} %copy-done, f32[2,4,256]{2,1,0:T(4,128)S(1)} %bitcast.228, pred[256,512]{0,1:T(8,128)(4,1)S(1)} %compare_and_fusion.5, f32[1,2,4,256,64]{3,4,2,1,0:T(8,128)S(1)} %get-tuple-element.487, ...), kind=kOutput, calls=%fused_computation.35.clone.1 | convolution fusion | flops 139853824 | bytes 5521409 | tf_op jit(solution)/shard_map/while/body/eval_jaxpr/gkrbs,gskh->gkrbh/dot_general | solution.py:98
  177.9 1.9 copy-done
  179.9 1.0 fusion.100
  180.9 3.4 %fusion.101 = f32[1,2,4,256,64]{3,4,2,1,0:T(8,128)S(1)} fusion(bf16[512,2,64,1]{0,2,3,1:T(8,128)(2,1)S(1)} %bitcast.229, f32[2,512,256,4]{2,1,3,0:T(8,128)} %copy-done, f32[2,4,256]{2,1,0:T(4,128)S(1)} %bitcast.228, pred[256,512]{0,1:T(8,128)(4,1)S(1)} %compare_and_fusion.5, f32[1,2,4,256,64]{3,4,2,1,0:T(8,128)S(1)} %get-tuple-element.487, ...), kind=kOutput, calls=%fused_computation.35.clone.1 | convolution fusion | flops 139853824 | bytes 5521409 | tf_op jit(solution)/shard_map/while/body/eval_jaxpr/gkrbs,gskh->gkrbh/dot_general | solution.py:98
  186.5 1.9 copy-done
  188.5 1.0 fusion.100
  189.5 3.4 %fusion.101 = f32[1,2,4,256,64]{3,4,2,1,0:T(8,128)S(1)} fusion(bf16[512,2,64,1]{0,2,3,1:T(8,128)(2,1)S(1)} %bitcast.229, f32[2,512,256,4]{2,1,3,0:T(8,128)} %copy-done, f32[2,4,256]{2,1,0:T(4,128)S(1)} %bitcast.228, pred[256,512]{0,1:T(8,128)(4,1)S(1)} %compare_and_fusion.5, f32[1,2,4,256,64]{3,4,2,1,0:T(8,128)S(1)} %get-tuple-element.487, ...), kind=kOutput, calls=%fused_computation.35.clone.1 | convolution fusion | flops 139853824 | bytes 5521409 | tf_op jit(solution)/shard_map/while/body/eval_jaxpr/gkrbs,gskh->gkrbh/dot_general | solution.py:98
  195.2 1.9 copy-done
  197.1 1.0 fusion.100
  198.1 3.4 %fusion.101 = f32[1,2,4,256,64]{3,4,2,1,0:T(8,128)S(1)} fusion(bf16[512,2,64,1]{0,2,3,1:T(8,128)(2,1)S(1)} %bitcast.229, f32[2,512,256,4]{2,1,3,0:T(8,128)} %copy-done, f32[2,4,256]{2,1,0:T(4,128)S(1)} %bitcast.228, pred[256,512]{0,1:T(8,128)(4,1)S(1)} %compare_and_fusion.5, f32[1,2,4,256,64]{3,4,2,1,0:T(8,128)S(1)} %get-tuple-element.487, ...), kind=kOutput, calls=%fused_computation.35.clone.1 | convolution fusion | flops 139853824 | bytes 5521409 | tf_op jit(solution)/shard_map/while/body/eval_jaxpr/gkrbs,gskh->gkrbh/dot_general | solution.py:98
  203.8 1.9 copy-done
  205.7 1.0 fusion.100
  206.8 3.4 %fusion.101 = f32[1,2,4,256,64]{3,4,2,1,0:T(8,128)S(1)} fusion(bf16[512,2,64,1]{0,2,3,1:T(8,128)(2,1)S(1)} %bitcast.229, f32[2,512,256,4]{2,1,3,0:T(8,128)} %copy-done, f32[2,4,256]{2,1,0:T(4,128)S(1)} %bitcast.228, pred[256,512]{0,1:T(8,128)(4,1)S(1)} %compare_and_fusion.5, f32[1,2,4,256,64]{3,4,2,1,0:T(8,128)S(1)} %get-tuple-element.487, ...), kind=kOutput, calls=%fused_computation.35.clone.1 | convolution fusion | flops 139853824 | bytes 5521409 | tf_op jit(solution)/shard_map/while/body/eval_jaxpr/gkrbs,gskh->gkrbh/dot_general | solution.py:98
  212.4 1.9 copy-done
  214.3 1.0 fusion.100
  215.4 3.4 %fusion.101 = f32[1,2,4,256,64]{3,4,2,1,0:T(8,128)S(1)} fusion(bf16[512,2,64,1]{0,2,3,1:T(8,128)(2,1)S(1)} %bitcast.229, f32[2,512,256,4]{2,1,3,0:T(8,128)} %copy-done, f32[2,4,256]{2,1,0:T(4,128)S(1)} %bitcast.228, pred[256,512]{0,1:T(8,128)(4,1)S(1)} %compare_and_fusion.5, f32[1,2,4,256,64]{3,4,2,1,0:T(8,128)S(1)} %get-tuple-element.487, ...), kind=kOutput, calls=%fused_computation.35.clone.1 | convolution fusion | flops 139853824 | bytes 5521409 | tf_op jit(solution)/shard_map/while/body/eval_jaxpr/gkrbs,gskh->gkrbh/dot_general | solution.py:98
  221.0 1.9 copy-done
  223.0 1.0 fusion.100
  224.0 3.4 %fusion.101 = f32[1,2,4,256,64]{3,4,2,1,0:T(8,128)S(1)} fusion(bf16[512,2,64,1]{0,2,3,1:T(8,128)(2,1)S(1)} %bitcast.229, f32[2,512,256,4]{2,1,3,0:T(8,128)} %copy-done, f32[2,4,256]{2,1,0:T(4,128)S(1)} %bitcast.228, pred[256,512]{0,1:T(8,128)(4,1)S(1)} %compare_and_fusion.5, f32[1,2,4,256,64]{3,4,2,1,0:T(8,128)S(1)} %get-tuple-element.487, ...), kind=kOutput, calls=%fused_computation.35.clone.1 | convolution fusion | flops 139853824 | bytes 5521409 | tf_op jit(solution)/shard_map/while/body/eval_jaxpr/gkrbs,gskh->gkrbh/dot_general | solution.py:98
  227.5 1.8 copy.33
  229.2 27.5 %while.34 = (s32[]{:T(128)}, f32[1,2,4,256]{3,2,1,0:T(4,128)S(1)}, f32[1,2,4,256]{3,2,1,0:T(4,128)S(1)}, f32[1,2,4,256,64]{3,4,2,1,0:T(8,128)S(1)}, s32[8,512]{1...) while((s32[]{:T(128)}, f32[1,2,4,256]{3,2,1,0:T(4,128)S(1)}, ...), condition=%wide.region_8.9_spmd.clone, body=%wide.region_5.8_spmd.clone.sunk | while | flops 282728960 | bytes 15870065 | solution.py:117
  231.4 1.3 fusion.93
  233.8 1.0 fusion.92
  234.8 1.3 fusion.93
  238.3 1.3 fusion.93
  240.7 1.0 fusion.92
  241.7 1.3 fusion.93
  245.1 1.3 fusion.93
  247.5 1.0 fusion.92
  248.6 1.3 fusion.93
  252.0 1.3 fusion.93
  255.5 1.3 fusion.93
  256.9 20.7 %all-gather.14.cloned.1.call-done = bf16[2048,512]{1,0:T(8,128)(2,1)} async-done(((bf16[32,512]{1,0:T(8,128)(2,1)}), bf16[2048,512]{1,0:T(8,128)(2,1)}) %all-gather.14.cloned.1.call-update) | async-done | bytes 2097168 | tf_op jit(solution)/shard_map/all_gather | solution.py:144
  277.5 3.3 %fusion.42 = bf16[1,256,2048]{2,1,0:T(8,128)(2,1)} fusion(bf16[256,512]{0,1:T(8,128)(2,1)S(1)} %fusion.50, bf16[2048,512]{1,0:T(8,128)(2,1)} %all-gather.14.cloned.1.call-done), kind=kOutput, calls=%fused_computation.55 | convolution fusion | flops 537395200 | bytes 3407872 | tf_op jit(solution)/shard_map/dot_general | solution.py:142
  280.9 24.9 %reduce-scatter.2.cloned.1.call-done = bf16[1,256,512]{2,1,0:T(8,128)(2,1)} async-done(((bf16[1,256,2048]{2,1,0:T(8,128)(2,1)}), bf16[1,256,512]{2,1,0:T(8,128)(2,1)}) %reduce-scatter.2.cloned.1.call-update) | async-done | bytes 262160 | tf_op jit(solution)/shard_map/reduce_scatter | solution.py:149
  (206 shorter events, 36.1 us)
Async XLA Ops:
  6.5 105.2 %all-gather.8.cloned.1.call-start = ((), (), s32[]{:S(2)}) async-start(), calls=%async_computation.2 | async-start | bytes 1310720 | tf_op jit(solution)/shard_map/all_gather | solution.py:44
  7.3 111.0 %all-gather.10.cloned.1.call-start = ((), (), s32[]{:S(2)}) async-start(), calls=%async_computation.3 | async-start | bytes 2129920 | tf_op jit(solution)/shard_map/all_gather | solution.py:53
  8.0 150.4 %all-gather.6.cloned.1.call-start = ((), (), s32[]{:S(2)}) async-start(), calls=%async_computation.1 | async-start | bytes 2228224 | tf_op jit(solution)/shard_map/all_gather | solution.py:129
  9.6 107.8 %copy-start.2 = (f32[8]{0:T(128)S(1)}, f32[8]{0:T(128)}, u32[]{:S(2)}) copy-start(f32[8]{0:T(128)} %param.21) | copy-start | bytes 100
  9.6 217.8 %all-gather.12.cloned.1.call-start = ((), (), s32[]{:S(2)}) async-start(), calls=%async_computation.4 | async-start | bytes 2228224 | tf_op jit(solution)/shard_map/all_gather | solution.py:130
  111.8 3.5 %copy-start.1 = (bf16[1,256,2048]{2,1,0:T(8,128)(2,1)S(1)}, bf16[1,256,2048]{2,1,0:T(8,128)(2,1)}, u32[]{:S(2)}) copy-start(bf16[1,256,2048]{2,1,0:T(8,128)(2,1)} %all-gather.8.cloned.1.call-done) | copy-start | bytes 3145732
  116.5 161.0 %all-gather.14.cloned.1.call-start = ((), (), s32[]{:S(2)}) async-start(), calls=%async_computation.5 | async-start | bytes 2129920 | tf_op jit(solution)/shard_map/all_gather | solution.py:144
  117.1 188.7 %reduce-scatter.2.cloned.1.call-start = ((), (), s32[]{:S(2)}) async-start(), calls=%async_computation.6 | async-start | bytes 1310720 | tf_op jit(solution)/shard_map/reduce_scatter | solution.py:149
  160.7 2.0 copy-start
  169.3 2.0 copy-start
  177.9 2.0 copy-start
  186.5 2.0 copy-start
  195.1 2.0 copy-start
  203.8 2.0 copy-start
  212.4 2.0 copy-start
  221.0 2.0 copy-start
Sparse Core Ops, SparseCore 0:
  9.2 29.4 all-gather.7
  41.5 76.7 all-gather.9
  120.1 38.3 all-gather.5
  160.1 39.2 all-gather.11
  202.0 75.5 all-gather.13
  281.0 24.7 reduce-scatter.1
where the time goes:
time: 314 us; the launch traced here: 313 us
  blocking collectives  101 us (32%)
  waiting for transfers between devices  85.1 us (27%)
  matrix products  58.7 us (19%)
  local copies, waits for them, and re-layouts  27.1 us (9%)
  other arithmetic  24.6 us (8%)
  between operations  14.3 us (5%)
    all_gather x1, blocking collectives, on_device(): lax.all_gather(w_value, ('grp', 'tok'), axis=0, tiled=True)  52.9 us
    all_gather x1, blocking collectives, on_device(): lax.all_gather(w_key, ('grp', 'tok'), axis=0, tiled=True)  48.3 us
    all_gather x1, waiting for transfers between devices, on_device(): lax.all_gather(kv_prefix, 'tok', axis=1, tiled=True)  37.4 us
    dot_general x16, matrix products, attend_part(): jnp.einsum('gkrbs,gskh->gkrbh', expo_terms.astype(jnp.bfloat16), value_ro...  37.4 us
    reduce_scatter x1, waiting for transfers between devices, on_device(): lax.psum_scatter(partial_out.astype(jnp.bfloat16), 'mdl', scatter_dimensi...  24.9 us
    all_gather x1, waiting for transfers between devices, on_device(): lax.all_gather(w_out, ('grp', 'tok'), axis=0, tiled=True)  20.7 us
    reduce_sum x16, other arithmetic, attend_part(): denoms = denoms * rescale + jnp.sum(expo_terms, axis=-1)  16.2 us
    while x32, local copies, waits for them, and re-layouts  15.5 us
  transfers between devices with their start and end apart: 6, of which 4 were waited for; matrix products, arithmetic and copies ran while one was open for 29% of the time, Pallas kernels for 0%

commit v1 on v0

--- a/solution.py
+++ b/solution.py
@@ -7,6 +7,12 @@
 SCORE_SCALE = 0.015625
 EPSILON = 1e-05
 LOG_THETA = 16.11809565095832
+
+
+def tiled_gather(x, axis, dim):
+    size = lax.axis_size(axis)
+    repeats = [size if d == dim else 1 for d in range(x.ndim)]
+    return lax.all_to_all(jnp.tile(x, repeats), axis, split_axis=dim, concat_axis=dim, tiled=True)
 
 
 def rotate(heads_in, positions):
@@ -126,7 +132,7 @@
     )
     softmax_state = initial_state
     shard_pair = (
-        lax.all_gather(kv_prefix, "tok", axis=1, tiled=True),
+        tiled_gather(kv_prefix, "tok", 1),
         lax.all_gather(kv_new, "tok", axis=1, tiled=True),
     )
     row_count = shard_pair[0].shape[1]

time: 314 us -> 373 us (1.19)
  local copies, waits for them, and re-layouts: 27.1 us -> 53.2 us
  other arithmetic: 24.6 us -> 46.3 us
  matrix products: 58.7 us -> 75.9 us
  waiting for transfers between devices: 85.1 us -> 74.3 us
  starting transfers between devices: 0.38 us -> 4.99 us
    all_to_all x0 -> x1, waiting for transfers between devices: none -> 47.1 us  [tiled_gather(): lax.all_to_all(jnp.tile(x, repeats), axis, split_axis=dim, concat_axis=di...]
    all_gather x1 -> x0, waiting for transfers between devices: 37.4 us -> none  [on_device(): lax.all_gather(kv_prefix, 'tok', axis=1, tiled=True)]
    another operation x0 -> x2, local copies, waits for them, and re-layouts: none -> 25.2 us  [tiled_gather(): jnp.tile(x, repeats)]
    unnamed x2 -> x3, other arithmetic: 0.01 us -> 21.6 us
    all_gather x1, waiting for transfers between devices: 20.7 us -> 0.02 us  [on_device(): lax.all_gather(w_out, ('grp', 'tok'), axis=0, tiled=True)]
    dot_general x16, matrix products: 13 us -> 28.6 us  [attend_part(): jnp.einsum('gbkrh,gskh->gkrbs', query_groups, key_rows, preferred_element...]
    while x32 -> x64, local copies, waits for them, and re-layouts: 15.5 us -> 0.14 us
    unnamed x4 -> x16, local copies, waits for them, and re-layouts: 0.01 us -> 11.9 us
  transfers between devices with their start and end apart: 6 -> 6, of which waited for: 4 -> 2; matrix products, arithmetic and copies ran while one was open for 29% -> 46% of each run, Pallas kernels for 0% -> 0%
where the time goes in v1:
time: 373 us; the launch traced here: 372 us
  blocking collectives  101 us (27%)
  matrix products  75.9 us (20%)
  waiting for transfers between devices  74.3 us (20%)
  local copies, waits for them, and re-layouts  53.2 us (14%)
  other arithmetic  46.3 us (12%)
  between operations  14.1 us (4%)
  starting transfers between devices  4.99 us (1%)
    all_gather x1, blocking collectives, on_device(): lax.all_gather(w_key, ('grp', 'tok'), axis=0, tiled=True)  52.9 us
    all_gather x1, blocking collectives, on_device(): lax.all_gather(w_value, ('grp', 'tok'), axis=0, tiled=True)  48.5 us
    all_to_all x1, waiting for transfers between devices, tiled_gather(): lax.all_to_all(jnp.tile(x, repeats), axis, split_axis=dim, concat_axis=di...  47.1 us
    dot_general x16, matrix products, attend_part(): jnp.einsum('gkrbs,gskh->gkrbh', expo_terms.astype(jnp.bfloat16), value_ro...  38.6 us
    dot_general x16, matrix products, attend_part(): jnp.einsum('gbkrh,gskh->gkrbs', query_groups, key_rows, preferred_element...  28.6 us
    another operation x2, local copies, waits for them, and re-layouts, tiled_gather(): jnp.tile(x, repeats)  25.2 us
    reduce_scatter x1, waiting for transfers between devices, on_device(): lax.psum_scatter(partial_out.astype(jnp.bfloat16), 'mdl', scatter_dimensi...  25.1 us
    unnamed x3, other arithmetic  21.6 us
  transfers between devices with their start and end apart: 6, of which 2 were waited for; matrix products, arithmetic and copies ran while one was open for 46% of the time, Pallas kernels for 0%

profile of v1, /device:TPU:2, one launch (start us, length us, event | category | flops | bytes accessed | tf_op | source)
XLA Modules:
  0.0 371.5 jit_solution(14840170086851981876)
XLA Ops:
  9.0 52.9 %all_gather.20 = bf16[2048,128]{1,0:T(8,128)(2,1)S(1)} all-gather(bf16[32,128]{1,0:T(8,128)(2,1)} %param.18), channel_id=1, replica_groups=mesh['grp'=4,'tok'=16,'mdl'=4] {'grp','tok'}, dimensions={0}, use_global_device_ids=true | all-gather | bytes 532480 | tf_op jit(solution)/shard_map/all_gather | solution.py:60
  61.9 48.5 %all_gather.21 = bf16[2048,128]{1,0:T(8,128)(2,1)S(1)} all-gather(bf16[32,128]{1,0:T(8,128)(2,1)} %param.19), channel_id=1, replica_groups=mesh['grp'=4,'tok'=16,'mdl'=4] {'grp','tok'}, dimensions={0}, use_global_device_ids=true | all-gather | bytes 532480 | tf_op jit(solution)/shard_map/all_gather | solution.py:61
  110.3 1.6 fusion.43
  111.9 1.8 fusion.55
  115.3 25.0 %copy.49 = bf16[1,4096,256]{2,0,1:T(2,128)(2,1)} copy(bf16[1,4096,256]{2,1,0:T(8,128)(2,1)S(1)} %bitcast.233) | data formatting | bytes 4194304 | tf_op jit(solution)/shard_map/tile | solution.py:15
  140.9 21.6 %reduce.17 = bf16[4096,256]{1,0:T(8,128)(2,1)S(1)} reduce(bf16[4096,1,256]{2,1,0:T(2,128)(2,1)} %bitcast.229, bf16[]{:T(256)} %broadcast.177), dimensions={1}, to_apply=%bitcast.166.reduce_sub_computation | reduce | bytes 4194306
  162.5 2.1 reshape.352
  164.6 4.6 %all-to-all-start = ((bf16[16,2,32768]{2,1,0:T(2,128)(2,1)}), bf16[16,2,32768]{2,1,0:T(2,128)(2,1)S(1)}, u32[]{:S(2)}, u32[]{:S(2)}) async-start(bf16[16,2,32768]{2,1,0:T(2,128)(2,1)} %reshape.352), calls=%async_computation | async-start | bytes 4194304 | tf_op jit(solution)/shard_map/all_to_all | solution.py:15
  172.5 47.1 %all-to-all-done = bf16[16,2,32768]{2,1,0:T(2,128)(2,1)S(1)} async-done(((bf16[16,2,32768]{2,1,0:T(2,128)(2,1)}), bf16[16,2,32768]{2,1,0:T(2,128)(2,1)S(1)}, u32[]{:S(2)}, u32[]{:S(2)}) %all-to-all-start) | async-done | bytes 2097184 | tf_op jit(solution)/shard_map/all_to_all | solution.py:15
  219.6 6.7 %reshape.353 = bf16[4096,1,256]{2,1,0:T(2,128)(2,1)} reshape(bf16[16,2,32768]{2,1,0:T(2,128)(2,1)S(1)} %all-to-all-done) | data formatting | bytes 4194304
  226.4 2.5 copy.44
  228.9 2.9 fusion.57
  232.1 69.1 %while.35 = (s32[]{:T(128)}, f32[1,2,4,256]{3,2,1,0:T(4,128)S(1)}, f32[1,2,4,256]{3,2,1,0:T(4,128)S(1)}, f32[1,2,4,256,64]{3,4,2,1,0:T(8,128)}, s32[8,512]{1,0:T...) while((s32[]{:T(128)}, f32[1,2,4,256]{3,2,1,0:T(4,128)S(1)}, ...), condition=%wide.region_4.5_spmd.clone, body=%wide.region_1.4_spmd.clone.sunk | while | flops 282862080 | bytes 37365964 | solution.py:123
  233.3 2.8 fusion.98
  236.1 3.5 fusion.101
  239.7 1.0 fusion.100
  241.9 2.8 fusion.98
  244.7 3.5 fusion.101
  248.3 1.0 fusion.100
  250.6 2.8 fusion.98
  253.4 3.6 fusion.101
  256.9 1.0 fusion.100
  259.2 2.8 fusion.98
  262.0 3.6 fusion.101
  265.6 1.0 fusion.100
  267.8 2.8 fusion.98
  270.7 3.5 fusion.101
  274.2 1.0 fusion.100
  276.5 2.8 fusion.98
  279.3 3.5 fusion.101
  282.9 1.0 fusion.100
  285.1 2.8 fusion.98
  287.9 3.5 fusion.101
  291.5 1.0 fusion.100
  293.8 2.8 fusion.98
  296.6 3.5 fusion.101
  301.2 1.8 copy.48
  303.1 33.2 %while.34 = (s32[]{:T(128)}, f32[1,2,4,256]{3,2,1,0:T(4,128)S(1)}, f32[1,2,4,256]{3,2,1,0:T(4,128)S(1)}, f32[1,2,4,256,64]{3,4,2,1,0:T(8,128)S(1)}, s32[8,512]{1...) while((s32[]{:T(128)}, f32[1,2,4,256]{3,2,1,0:T(4,128)S(1)}, ...), condition=%wide.region_8.9_spmd.clone, body=%wide.region_5.8_spmd.clone.sunk | while | flops 282728960 | bytes 15870057 | solution.py:123
  304.9 1.3 fusion.93
  309.1 1.3 fusion.93
  313.2 1.3 fusion.93
  317.4 1.3 fusion.93
  321.5 1.3 fusion.93
  325.7 1.3 fusion.93
  329.8 1.3 fusion.93
  334.0 1.3 fusion.93
  336.5 3.3 fusion.42
  339.8 25.1 %reduce-scatter.2.cloned.1.call-done = bf16[1,256,512]{2,1,0:T(8,128)(2,1)} async-done(((bf16[1,256,2048]{2,1,0:T(8,128)(2,1)}), bf16[1,256,512]{2,1,0:T(8,128)(2,1)}) %reduce-scatter.2.cloned.1.call-update) | async-done | bytes 262160 | tf_op jit(solution)/shard_map/reduce_scatter | solution.py:155
  (252 shorter events, 40.5 us)
Async XLA Ops:
  6.5 103.8 %all-gather.5.cloned.1.call-start = ((), (), s32[]{:S(2)}) async-start(), calls=%async_computation.2 | async-start | bytes 1310720 | tf_op jit(solution)/shard_map/all_gather | solution.py:50
  7.3 107.8 %copy-start.5 = (bf16[1,256,128]{2,1,0:T(8,128)(2,1)S(1)}, bf16[1,256,128]{2,1,0:T(8,128)(2,1)}, u32[]{:S(2)}) copy-start(bf16[1,256,128]{2,1,0:T(8,128)(2,1)} %param.23) | copy-start | bytes 196612
  7.3 107.8 %copy-start.6 = (bf16[1,256,128]{2,1,0:T(8,128)(2,1)S(1)}, bf16[1,256,128]{2,1,0:T(8,128)(2,1)}, u32[]{:S(2)}) copy-start(bf16[1,256,128]{2,1,0:T(8,128)(2,1)} %param.22) | copy-start | bytes 196612
  7.3 221.7 %all-gather.7.cloned.1.call-start = ((), (), s32[]{:S(2)}) async-start(), calls=%async_computation.3 | async-start | bytes 2129920 | tf_op jit(solution)/shard_map/all_gather | solution.py:59
  8.0 293.2 %all-gather.9.cloned.1.call-start = ((), (), s32[]{:S(2)}) async-start(), calls=%async_computation.4 | async-start | bytes 2228224 | tf_op jit(solution)/shard_map/all_gather | solution.py:136
  110.3 3.5 copy-start.1
  162.5 7.6 %copy-start.8 = (f32[8]{0:T(128)S(1)}, f32[8]{0:T(128)}, u32[]{:S(2)}) copy-start(f32[8]{0:T(128)} %param.21) | copy-start | bytes 100
  164.6 55.1 %all-to-all-start = ((bf16[16,2,32768]{2,1,0:T(2,128)(2,1)}), bf16[16,2,32768]{2,1,0:T(2,128)(2,1)S(1)}, u32[]{:S(2)}, u32[]{:S(2)}) async-start(bf16[16,2,32768]{2,1,0:T(2,128)(2,1)} %reshape.352), calls=%async_computation | async-start | bytes 4194304 | tf_op jit(solution)/shard_map/all_to_all | solution.py:15
  169.2 167.3 %all-gather.11.cloned.1.call-start = ((), (), s32[]{:S(2)}) async-start(), calls=%async_computation.5 | async-start | bytes 2129920 | tf_op jit(solution)/shard_map/all_gather | solution.py:150
  169.8 195.2 %reduce-scatter.2.cloned.1.call-start = ((), (), s32[]{:S(2)}) async-start(), calls=%async_computation.6 | async-start | bytes 1310720 | tf_op jit(solution)/shard_map/reduce_scatter | solution.py:155
  232.1 4.0 %copy-start.2 = (f32[1,2,4,256,64]{3,4,2,1,0:T(8,128)S(1)}, f32[1,2,4,256,64]{3,4,2,1,0:T(8,128)}, u32[]{:S(2)}) copy-start(f32[1,2,4,256,64]{3,4,2,1,0:T(8,128)} %get-tuple-element.519) | copy-start | bytes 1572868 | tf_op jit(solution)/shard_map/while
  236.1 3.6 copy-start
  239.6 1.1 copy-start.3
  240.7 4.0 %copy-start.2 = (f32[1,2,4,256,64]{3,4,2,1,0:T(8,128)S(1)}, f32[1,2,4,256,64]{3,4,2,1,0:T(8,128)}, u32[]{:S(2)}) copy-start(f32[1,2,4,256,64]{3,4,2,1,0:T(8,128)} %get-tuple-element.519) | copy-start | bytes 1572868 | tf_op jit(solution)/shard_map/while
  244.7 3.6 copy-start
  248.3 1.1 copy-start.3
  249.4 4.0 %copy-start.2 = (f32[1,2,4,256,64]{3,4,2,1,0:T(8,128)S(1)}, f32[1,2,4,256,64]{3,4,2,1,0:T(8,128)}, u32[]{:S(2)}) copy-start(f32[1,2,4,256,64]{3,4,2,1,0:T(8,128)} %get-tuple-element.519) | copy-start | bytes 1572868 | tf_op jit(solution)/shard_map/while
  253.3 3.6 copy-start
  256.9 1.1 copy-start.3
  258.0 4.0 %copy-start.2 = (f32[1,2,4,256,64]{3,4,2,1,0:T(8,128)S(1)}, f32[1,2,4,256,64]{3,4,2,1,0:T(8,128)}, u32[]{:S(2)}) copy-start(f32[1,2,4,256,64]{3,4,2,1,0:T(8,128)} %get-tuple-element.519) | copy-start | bytes 1572868 | tf_op jit(solution)/shard_map/while
  262.0 3.6 copy-start
  265.6 1.1 copy-start.3
  266.7 4.0 %copy-start.2 = (f32[1,2,4,256,64]{3,4,2,1,0:T(8,128)S(1)}, f32[1,2,4,256,64]{3,4,2,1,0:T(8,128)}, u32[]{:S(2)}) copy-start(f32[1,2,4,256,64]{3,4,2,1,0:T(8,128)} %get-tuple-element.519) | copy-start | bytes 1572868 | tf_op jit(solution)/shard_map/while
  270.6 3.6 copy-start
  274.2 1.1 copy-start.3
  275.3 4.0 %copy-start.2 = (f32[1,2,4,256,64]{3,4,2,1,0:T(8,128)S(1)}, f32[1,2,4,256,64]{3,4,2,1,0:T(8,128)}, u32[]{:S(2)}) copy-start(f32[1,2,4,256,64]{3,4,2,1,0:T(8,128)} %get-tuple-element.519) | copy-start | bytes 1572868 | tf_op jit(solution)/shard_map/while
  279.3 3.6 copy-start
  282.8 1.1 copy-start.3
  283.9 4.0 %copy-start.2 = (f32[1,2,4,256,64]{3,4,2,1,0:T(8,128)S(1)}, f32[1,2,4,256,64]{3,4,2,1,0:T(8,128)}, u32[]{:S(2)}) copy-start(f32[1,2,4,256,64]{3,4,2,1,0:T(8,128)} %get-tuple-element.519) | copy-start | bytes 1572868 | tf_op jit(solution)/shard_map/while
  287.9 3.6 copy-start
  291.5 1.1 copy-start.3
  292.6 4.0 %copy-start.2 = (f32[1,2,4,256,64]{3,4,2,1,0:T(8,128)S(1)}, f32[1,2,4,256,64]{3,4,2,1,0:T(8,128)}, u32[]{:S(2)}) copy-start(f32[1,2,4,256,64]{3,4,2,1,0:T(8,128)} %get-tuple-element.519) | copy-start | bytes 1572868 | tf_op jit(solution)/shard_map/while
  296.5 3.6 copy-start
  300.1 1.1 copy-start.3
  301.2 1.9 copy-start.4
  303.1 33.3 %copy-start.7 = (pred[256]{0:T(512)(128)(4,1)S(1)}, pred[256]{0:T(512)(128)(4,1)}, u32[]{:S(2)}) copy-start(pred[256]{0:T(512)(128)(4,1)} %fusion.53) | copy-start | bytes 772
Sparse Core Ops, SparseCore 0:
  9.2 29.4 all-gather.4
  41.5 76.6 all-gather.6
  119.9 39.5 all-gather.8
  172.5 91.1 all-gather.10
  340.0 24.9 reduce-scatter.1
